TPU v7x, 128 devices: a whole 4x4x4 slice. The times are simulated.
128 devices in a mesh: tok: 16 (over z, x), exp: 8 (over y, core).
Axes of the slice: x: 4, y: 4, z: 4, core: 2. Of those that a mesh axis runs over, the one named last changes fastest.
Arguments:
- tokens: bfloat16 [3072, 2048], P('tok'), may hold values from -6 to 6
- gain_attn: float32 [2048], replicated, may hold values from 0.5 to 1.5
- router_attn: bfloat16 [2048, 8], replicated, may hold values from -0.125 to 0.125
- kv_weight: bfloat16 [2048, 4096], P(None, 'exp')
- query_weight: bfloat16 [8, 2048, 2048], P('exp', None, 'tok')
- out_weight: bfloat16 [8, 2048, 2048], P('exp', 'tok'), may hold values from -0.125 to 0.125
- gain_mlp: float32 [2048], replicated, may hold values from 0.5 to 1.5
- router_mlp: bfloat16 [2048, 8], replicated, may hold values from -0.125 to 0.125
- gate_weight: bfloat16 [8, 2048, 5632], P('exp', None, 'tok'), may hold values from -0.125 to 0.125
- up_weight: bfloat16 [8, 2048, 5632], P('exp', None, 'tok'), may hold values from -0.125 to 0.125
- down_weight: bfloat16 [8, 5632, 2048], P('exp', 'tok'), may hold values from -0.078125 to 0.078125
- routes_attn: int32 [3072, 2], P('tok'), may hold values from 0 to 7, all different within a row; in each aligned block of 192 rows (0 to 191, 192 to 383, ...) at most 96 rows name the same one
- routes_mlp: int32 [3072, 2], P('tok'), may hold values from 0 to 7, all different within a row; in each aligned block of 192 rows (0 to 191, 192 to 383, ...) at most 96 rows name the same one
- lengths: int32 [3], replicated, may hold values from 256 to 1536, as said below
- page_table: int32 [3, 12, 2], replicated, may hold values from 0 to 15, as said below
Outputs:
- mixed: bfloat16 [3072, 2048], P('tok', 'exp')
- kv_pages: bfloat16 [32, 128, 4096], P('tok', None, 'exp')
Inputs may be any that keep to these rules, and one draw needn't show every extreme that they name: `routes_attn`: in each device's block of 192 tokens no expert is named by more than 96 tokens, a bound that some block reaches of them. `routes_mlp`: in each device's block of 192 tokens no expert is named by more than 96 tokens, a bound that some block reaches of them. The lengths sum to 3072; one prompt has exactly 1536 tokens. `page_table`: entry [s, i] holds (owner along tok, slot) of page i of prompt s, its tokens i * 128 to (i + 1) * 128 - 1; existing pages have distinct (owner, slot) pairs; the pages touched by one device's block of 192 tokens have distinct owners, so one block sends at most one page's tokens to an owner; entries past a prompt's last page are 0.
All inputs are finite; a program needn't handle non-finite values.
Results may differ from a plain program's by a relative error of at most 0.015.
The roundings to bfloat16 on the way count: a program that leaves them out, or rounds other values in their place, can miss the bound.
Values may be sent and summed in bfloat16 or wider, within the bound.
A program may use at most 128 MiB of HBM per device.

v0:
```python
import jax
import jax.numpy as jnp
from jax import lax
from jax.sharding import PartitionSpec as P

HD = 128
PAGE = 128
epsilon = 1e-06


def normalize(values, gain):
    return values * lax.rsqrt(jnp.mean(values * values, axis=-1, keepdims=True) + epsilon) * gain


def rotate(values, position):
    half_width = values.shape[-1] // 2
    exponent = jnp.arange(half_width, dtype=jnp.float32) * (2.0 / values.shape[-1])
    frequency = jnp.power(jnp.float32(10000.0), -exponent)
    angles = position.astype(jnp.float32)[:, None] * frequency[None, :]
    cosine = jnp.cos(angles)[:, None, :]
    sine_part = jnp.sin(angles)[:, None, :]
    leading = values[..., :half_width]
    trailing = values[..., half_width:]
    return jnp.concatenate(
        [leading * cosine - trailing * sine_part, trailing * cosine + leading * sine_part], axis=-1
    )


def locate(lengths, number):
    segment_ends = jnp.cumsum(lengths)
    segment_starts = segment_ends - lengths
    segment = jnp.sum((number[:, None] >= segment_ends[None, :]).astype(jnp.int32), axis=1)
    matched = segment[:, None] == jnp.arange(lengths.shape[0], dtype=jnp.int32)[None, :]
    start_of = jnp.sum(jnp.where(matched, segment_starts[None, :], 0), axis=1)
    return (segment, (number - start_of).astype(jnp.int32), start_of)


def pair_gates(logits, routes):
    leading = jnp.take_along_axis(logits, routes[:, 0:1], axis=1)[:, 0]
    trailing = jnp.take_along_axis(logits, routes[:, 1:2], axis=1)[:, 0]
    return (jax.nn.sigmoid(leading - trailing), jax.nn.sigmoid(trailing - leading))


def compact(routes, leading, trailing, expert, capacity):
    count_rows = routes.shape[0]
    chosen = (routes[:, 0] == expert) | (routes[:, 1] == expert)
    weight = jnp.where(routes[:, 0] == expert, leading, 0.0) + jnp.where(
        routes[:, 1] == expert, trailing, 0.0
    )
    ranking = jnp.cumsum(chosen.astype(jnp.int32)) - 1
    slot_rank = jnp.arange(capacity, dtype=jnp.int32)
    matches = chosen[None, :] & (ranking[None, :] == slot_rank[:, None])
    picked = jnp.sum(
        jnp.where(matches, jnp.arange(count_rows, dtype=jnp.int32)[None, :], 0), axis=1
    )
    filled = slot_rank < jnp.sum(chosen.astype(jnp.int32))
    return (picked, jnp.where(filled, jnp.take(weight, picked), 0.0))


def spread_rows(picked, contribution, count_rows):
    placing = (jnp.arange(count_rows, dtype=jnp.int32)[:, None] == picked[None, :]).astype(
        jnp.float32
    )
    return jnp.dot(placing, contribution, precision=lax.Precision.HIGHEST)


def attend(queries, query_number, query_segment, key_heads, value_heads, key_segment):
    query_total = queries.shape[0]
    key_total = key_heads.shape[0]
    query_groups = max(1, query_total // 512)
    query_rows = query_total // query_groups
    key_groups = max(1, key_total // 512)
    key_rows = key_total // key_groups
    score_scale = queries.shape[-1] ** (-0.5)
    heads_here = queries.shape[1]
    key_number = jnp.arange(key_total, dtype=jnp.int32)
    results = []
    for query_group in range(query_groups):
        row_begin = query_group * query_rows
        query_part = queries[row_begin : row_begin + query_rows]
        number_part = query_number[row_begin : row_begin + query_rows]
        segment_part = query_segment[row_begin : row_begin + query_rows]

        def visit(counter, running):
            highest, denominator, summed = running
            first_key = counter * key_rows
            key_part = lax.dynamic_slice_in_dim(key_heads, first_key, key_rows, 0)
            value_part = lax.dynamic_slice_in_dim(value_heads, first_key, key_rows, 0)
            segment_keys = lax.dynamic_slice_in_dim(key_segment, first_key, key_rows, 0)
            number_keys = lax.dynamic_slice_in_dim(key_number, first_key, key_rows, 0)
            allowed = (segment_keys[None, :] == segment_part[:, None]) & (
                number_keys[None, :] <= number_part[:, None]
            )
            scores = (
                jnp.einsum("qhd,khd->hqk", query_part, key_part, preferred_element_type=jnp.float32)
                * score_scale
            )
            scores = jnp.where(allowed[None], scores, -1e30)
            newest = jnp.maximum(highest, jnp.max(scores, axis=2))
            weights = jnp.where(allowed[None], jnp.exp(scores - newest[:, :, None]), 0.0)
            shrink = jnp.exp(highest - newest)
            denominator = denominator * shrink + jnp.sum(weights, axis=2)
            summed = summed * shrink[:, :, None] + jnp.einsum(
                "hqk,khd->hqd",
                weights.astype(jnp.bfloat16),
                value_part,
                preferred_element_type=jnp.float32,
            )
            return (newest, denominator, summed)

        start_state = (
            jnp.full((heads_here, query_rows), -1e30, jnp.float32),
            jnp.zeros((heads_here, query_rows), jnp.float32),
            jnp.zeros((heads_here, query_rows, queries.shape[-1]), jnp.float32),
        )
        highest, denominator, summed = lax.fori_loop(0, key_groups, visit, start_state)
        results.append(jnp.swapaxes((summed / denominator[:, :, None]).astype(jnp.bfloat16), 0, 1))
    return jnp.concatenate(results, axis=0)


def shards(
    tokens,
    gain_attn,
    router_attn,
    kv_weight,
    query_weight,
    out_weight,
    gain_mlp,
    router_mlp,
    gate_weight,
    up_weight,
    down_weight,
    routes_attn,
    routes_mlp,
    lengths,
    page_table,
):
    tok_count = lax.axis_size("tok")
    exp_count = lax.axis_size("exp")
    tok_rank = lax.axis_index("tok")
    exp_rank = lax.axis_index("exp")
    rows_here, model_width = tokens.shape
    head_size = HD
    heads_kv = kv_weight.shape[1] // (2 * head_size)
    heads_here = query_weight.shape[2] // head_size
    capacity = rows_here // 2
    total_tokens = rows_here * tok_count
    page_rows = PAGE
    pages_each = page_table.shape[1]
    slot_count = (total_tokens // page_rows + lengths.shape[0]) // tok_count + 1
    widened = tokens.astype(jnp.float32)
    normed = normalize(widened, gain_attn).astype(jnp.bfloat16)
    own_number = tok_rank * rows_here + jnp.arange(rows_here, dtype=jnp.int32)
    own_segment, own_offset, own_start = locate(lengths, own_number)
    projected_kv = jnp.dot(normed, kv_weight, preferred_element_type=jnp.float32).reshape(
        rows_here, heads_kv, 2, head_size
    )
    rotated = rotate(projected_kv[:, :, 0], own_offset)
    paired = (
        jnp.stack([rotated, projected_kv[:, :, 1]], axis=2)
        .astype(jnp.bfloat16)
        .reshape(rows_here, heads_kv * 2 * head_size)
    )
    entries = jnp.take(
        page_table.reshape(-1, 2), own_segment * pages_each + own_offset // page_rows, axis=0
    )
    owner_of = entries[:, 0]
    slot_of = entries[:, 1]
    placed = owner_of * page_rows + own_offset % page_rows
    selector = (
        jnp.arange(tok_count * page_rows, dtype=jnp.int32)[:, None] == placed[None, :]
    ).astype(jnp.bfloat16)
    outgoing = (
        jnp.dot(selector, paired, preferred_element_type=jnp.float32)
        .astype(jnp.bfloat16)
        .reshape(tok_count, page_rows, -1)
    )
    owner_hits = owner_of[None, :] == jnp.arange(tok_count, dtype=jnp.int32)[:, None]
    slot_sent = jnp.max(jnp.where(owner_hits, slot_of[None, :], 0), axis=1).reshape(tok_count, 1)
    arrived, arrived_slot = (
        lax.all_to_all(outgoing, "tok", split_axis=0, concat_axis=0, tiled=True),
        lax.all_to_all(slot_sent, "tok", split_axis=0, concat_axis=0, tiled=True),
    )
    filing = (
        jnp.arange(slot_count, dtype=jnp.int32)[:, None] == arrived_slot[:, 0][None, :]
    ).astype(jnp.bfloat16)
    kv_pages = (
        jnp.dot(filing, arrived.reshape(tok_count, -1), preferred_element_type=jnp.float32)
        .astype(jnp.bfloat16)
        .reshape(slot_count, page_rows, -1)
    )
    all_heads = lax.all_gather(paired, "exp", axis=1, tiled=True)
    regrouped = lax.all_to_all(
        all_heads.reshape(rows_here, tok_count, heads_here * 2 * head_size),
        "tok",
        split_axis=1,
        concat_axis=0,
        tiled=True,
    )
    regrouped = regrouped.reshape(total_tokens, heads_here, 2, head_size)
    key_heads = regrouped[:, :, 0]
    value_heads = regrouped[:, :, 1]
    key_segment, key_offset, key_start = locate(lengths, jnp.arange(total_tokens, dtype=jnp.int32))
    attn_logits = jnp.dot(normed, router_attn, preferred_element_type=jnp.float32)
    leading, trailing = pair_gates(attn_logits, routes_attn)
    picked, attn_gate = compact(routes_attn, leading, trailing, exp_rank, capacity)
    chosen_rows = jnp.take(normed, picked, axis=0)
    chosen_number = tok_rank * rows_here + picked
    query_full = jnp.dot(
        chosen_rows,
        lax.all_gather(query_weight[0], "tok", axis=1, tiled=True),
        preferred_element_type=jnp.float32,
    )
    chosen_segment, chosen_offset, chosen_start = locate(lengths, chosen_number)
    query_local = rotate(query_full.reshape(capacity, -1, head_size), chosen_offset).astype(
        jnp.bfloat16
    )
    number_copies = jnp.broadcast_to(chosen_number[:, None], (capacity, tok_count))
    query_heads, query_number = (
        lax.all_to_all(query_local, "tok", split_axis=1, concat_axis=0, tiled=True),
        lax.all_to_all(number_copies, "tok", split_axis=1, concat_axis=0, tiled=True),
    )
    query_number = query_number.reshape(-1)
    query_segment, query_offset, query_start = locate(lengths, query_number)
    attended = attend(query_heads, query_number, query_segment, key_heads, value_heads, key_segment)
    returned = lax.all_to_all(
        attended.reshape(tok_count, capacity, heads_here * head_size),
        "tok",
        split_axis=0,
        concat_axis=2,
        tiled=True,
    )
    returned = returned.reshape(capacity, -1)
    mixed_attn = jnp.dot(
        returned,
        lax.all_gather(out_weight[0], "tok", axis=0, tiled=True),
        preferred_element_type=jnp.float32,
    )
    attn_rows = spread_rows(picked, mixed_attn * attn_gate[:, None], rows_here)
    share_width = model_width // exp_count
    first_column = exp_rank * share_width
    attn_total = lax.psum(attn_rows.astype(jnp.bfloat16), "exp").astype(jnp.float32)
    residual = widened + attn_total
    normed_mlp = normalize(residual, gain_mlp).astype(jnp.bfloat16)
    residual_share = lax.dynamic_slice_in_dim(residual, first_column, share_width, 1)
    mlp_logits = jnp.dot(normed_mlp, router_mlp, preferred_element_type=jnp.float32)
    leading_mlp, trailing_mlp = pair_gates(mlp_logits, routes_mlp)
    picked_mlp, mlp_gate = compact(routes_mlp, leading_mlp, trailing_mlp, exp_rank, capacity)
    expert_input = jnp.take(normed_mlp, picked_mlp, axis=0)
    portion = lax.all_gather(expert_input, "tok", axis=0, tiled=True)
    gate_part = jnp.dot(portion, gate_weight[0], preferred_element_type=jnp.float32)
    upward = jnp.dot(portion, up_weight[0], preferred_element_type=jnp.float32)
    hidden = (jax.nn.silu(gate_part) * upward).astype(jnp.bfloat16)
    expert_out = lax.psum_scatter(
        jnp.dot(hidden, down_weight[0], preferred_element_type=jnp.float32).astype(jnp.bfloat16),
        "tok",
        scatter_dimension=0,
        tiled=True,
    ).astype(jnp.float32)
    expert_local = spread_rows(picked_mlp, expert_out * mlp_gate[:, None], rows_here)
    expert_share = lax.psum_scatter(
        expert_local.astype(jnp.bfloat16), "exp", scatter_dimension=1, tiled=True
    ).astype(jnp.float32)
    mixed = (residual_share + expert_share).astype(jnp.bfloat16)
    return (mixed, kv_pages)


def solution(mesh):
    return jax.shard_map(
        shards,
        mesh=mesh,
        in_specs=(
            P("tok", None),
            P(),
            P(),
            P(None, "exp"),
            P("exp", None, "tok"),
            P("exp", "tok", None),
            P(),
            P(),
            P("exp", None, "tok"),
            P("exp", None, "tok"),
            P("exp", "tok", None),
            P("tok", None),
            P("tok", None),
            P(),
            P(),
        ),
        out_specs=(P("tok", "exp"), P("tok", None, "exp")),
        check_vma=False,
    )
```

profile of v0, /device:TPU:0, one launch (start us, length us, event | category | flops | bytes accessed | tf_op | source)
XLA Modules:
  0.0 524.7 jit_solution(327691876324778887)
XLA Ops:
  18.7 8.0 %all-to-all-start = ((s32[96,16,1]{0,2,1:T(1,128)}), s32[96,16,1]{0,2,1:T(1,128)S(1)}, u32[]{:S(2)}, u32[]{:S(2)}) async-start(s32[96,16,1]{0,2,1:T(1,128)} %broadcast_in_dim.247), calls=%async_computation | async-start | bytes 16384 | tf_op jit(solution)/shard_map/all_to_all | solution.py:221
  32.3 11.2 %all-gather.7.cloned.1.call-done = bf16[192,4096]{1,0:T(8,128)(2,1)} async-done(((bf16[192,512]{1,0:T(8,128)(2,1)}), bf16[192,4096]{1,0:T(8,128)(2,1)}) %all-gather.7.cloned.1.call-update) | async-done | bytes 1572880 | tf_op jit(solution)/shard_map/all_gather | solution.py:192
  46.2 6.9 %all-to-all-start.1 = ((bf16[192,16,256]{2,0,1:T(8,128)(2,1)}), bf16[192,16,256]{2,0,1:T(8,128)(2,1)S(1)}, u32[]{:S(2)}, u32[]{:S(2)}) async-start(bf16[192,16,256]{2,0,1:T(8,128)(2,1)} %bitcast.202), calls=%async_computation.1 | async-start | bytes 3145728 | tf_op jit(solution)/shard_map/all_to_all | solution.py:193
  59.1 25.7 %all-to-all-done.1 = bf16[192,16,256]{2,0,1:T(8,128)(2,1)S(1)} async-done(((bf16[192,16,256]{2,0,1:T(8,128)(2,1)}), bf16[192,16,256]{2,0,1:T(8,128)(2,1)S(1)}, u32[]{:S(2)}, u32[]{:S(2)}) %all-to-all-start.1) | async-done | bytes 1572896 | tf_op jit(solution)/shard_map/all_to_all | solution.py:193
  88.3 3.5 fusion.139
  91.8 43.1 %all-gather.11.cloned.1.call-done = bf16[1,2048,2048]{2,1,0:T(8,128)(2,1)} async-done(((bf16[1,2048,128]{2,1,0:T(8,128)(2,1)}), bf16[1,2048,2048]{2,1,0:T(8,128)(2,1)}) %all-gather.11.cloned.1.call-update) | async-done | bytes 8388624 | tf_op jit(solution)/shard_map/all_gather | solution.py:211
  134.9 4.9 fusion.84
  141.7 5.0 all-to-all-start.2
  149.4 10.8 %all-to-all-done.2 = bf16[96,16,128]{2,0,1:T(8,128)(2,1)S(1)} async-done(((bf16[96,16,128]{2,0,1:T(8,128)(2,1)}), bf16[96,16,128]{2,0,1:T(8,128)(2,1)S(1)}, u32[]{:S(2)}, u32[]{:S(2)}) %all-to-all-start.2) | async-done | bytes 393248 | tf_op jit(solution)/shard_map/all_to_all | solution.py:220
  161.0 19.0 %while.54 = (s32[]{:T(128)}, f32[1,512]{1,0:T(1,128)S(1)}, f32[1,512]{1,0:T(1,128)S(1)}, f32[1,512,128]{2,1,0:T(8,128)}, s32[3072]{0:T(1024)S(1)}, /*index=5*/s3...) while((s32[]{:T(128)}, f32[1,512]{1,0:T(1,128)S(1)}, ...), condition=%wide.region_14.16_spmd.clone, body=%wide.region_11.15_spmd.clone.sunk | while | flops 139135488 | bytes 6226191 | solution.py:116
  181.1 14.5 %while.55 = (s32[]{:T(128)}, f32[1,512]{1,0:T(1,128)S(1)}, f32[1,512]{1,0:T(1,128)S(1)}, f32[1,512,128]{2,1,0:T(8,128)S(1)}, s32[3072]{0:T(1024)S(1)}, /*index=5...) while((s32[]{:T(128)}, f32[1,512]{1,0:T(1,128)S(1)}, ...), condition=%wide.region_18.20_spmd.clone, body=%wide.region_15.19_spmd.clone.sunk | while | flops 139135488 | bytes 4128983 | solution.py:116
  195.8 14.5 %while.56 = (s32[]{:T(128)}, f32[1,512]{1,0:T(1,128)S(1)}, f32[1,512]{1,0:T(1,128)S(1)}, f32[1,512,128]{2,1,0:T(8,128)S(1)}, s32[3072]{0:T(1024)S(1)}, /*index=5...) while((s32[]{:T(128)}, f32[1,512]{1,0:T(1,128)S(1)}, ...), condition=%wide.region_22.24_spmd.clone, body=%wide.region_19.23_spmd.clone.sunk | while | flops 139135488 | bytes 4128983 | solution.py:116
  211.3 3.6 all-to-all-start.3
  215.1 9.2 %all-to-all-done.3 = bf16[16,96,128]{2,1,0:T(8,128)(2,1)S(1)} async-done(((bf16[16,96,128]{2,1,0:T(8,128)(2,1)}), bf16[16,96,128]{2,1,0:T(8,128)(2,1)S(1)}, u32[]{:S(2)}, u32[]{:S(2)}) %all-to-all-start.3) | async-done | bytes 393248 | tf_op jit(solution)/shard_map/all_to_all | solution.py:226
  224.5 4.8 fusion.74
  231.8 58.7 %all-reduce.4.cloned.1.call-done = bf16[192,2048]{1,0:T(8,128)(2,1)} async-done(((bf16[192,2048]{1,0:T(8,128)(2,1)}), bf16[192,2048]{1,0:T(8,128)(2,1)}) %all-reduce.4.cloned.1.call-update) | async-done | bytes 786448 | tf_op jit(solution)/shard_map/psum | solution.py:242
  301.3 60.5 %all-gather.9.cloned.1.call-done = bf16[1536,2048]{1,0:T(8,128)(2,1)} async-done(((bf16[96,2048]{1,0:T(8,128)(2,1)}), bf16[1536,2048]{1,0:T(8,128)(2,1)}) %all-gather.9.cloned.1.call-update) | async-done | bytes 6291472 | tf_op jit(solution)/shard_map/all_gather | solution.py:250
  361.8 6.6 %fusion.82 = f32[1536,352]{0,1:T(8,128)} fusion(bf16[1536,2048]{1,0:T(8,128)(2,1)} %all-gather.9.cloned.1.call-done, bf16[1,2048,352]{1,2,0:T(8,128)(2,1)S(1)} %copy-done.33), kind=kOutput, calls=%fused_computation.123 | convolution fusion | flops 2214592512 | bytes 9895936 | tf_op jit(solution)/shard_map/dot_general | solution.py:251
  368.4 11.9 %convolution_convert_fusion.1 = bf16[1536,2048]{1,0:T(8,128)(2,1)} fusion(bf16[1,352,2048]{2,1,0:T(8,128)(2,1)S(1)} %copy-done.34, bf16[1536,2048]{1,0:T(8,128)(2,1)} %all-gather.9.cloned.1.call-done, f32[1536,352]{0,1:T(8,128)} %fusion.82, bf16[1,2048,352]{1,2,0:T(8,128)(2,1)} %param.36), kind=kOutput, calls=%fused_computation.104 | convolution fusion | flops 4435574784 | bytes 17629184 | tf_op jit(solution)/shard_map/dot_general | solution.py:255
  381.7 5.3 %all-to-all-start.4 = ((s32[16,1,1]{2,1,0:T(1,128)}), s32[16,1,1]{2,1,0:T(1,128)S(1)}, u32[]{:S(2)}, u32[]{:S(2)}) async-start(s32[16,1,1]{2,1,0:T(1,128)} %copy.66), calls=%async_computation.6 | async-start | bytes 16384 | tf_op jit(solution)/shard_map/all_to_all | solution.py:182
  389.1 5.4 %all-to-all-done.4 = s32[16,1,1]{2,1,0:T(1,128)S(1)} async-done(((s32[16,1,1]{2,1,0:T(1,128)}), s32[16,1,1]{2,1,0:T(1,128)S(1)}, u32[]{:S(2)}, u32[]{:S(2)}) %all-to-all-start.4) | async-done | bytes 96 | tf_op jit(solution)/shard_map/all_to_all | solution.py:182
  394.5 3.7 all-to-all-start.5
  398.3 83.9 %reduce-scatter.3.cloned.1.call-done = bf16[96,2048]{1,0:T(8,128)(2,1)} async-done(((bf16[1536,2048]{1,0:T(8,128)(2,1)}), bf16[96,2048]{1,0:T(8,128)(2,1)}) %reduce-scatter.3.cloned.1.call-update) | async-done | bytes 393232 | tf_op jit(solution)/shard_map/reduce_scatter | solution.py:254
  487.7 28.4 %reduce-scatter.5.cloned.1.call-done = bf16[192,256]{1,0:T(8,128)(2,1)} async-done(((bf16[192,2048]{1,0:T(8,128)(2,1)}), bf16[192,256]{1,0:T(8,128)(2,1)}) %reduce-scatter.5.cloned.1.call-update) | async-done | bytes 98320 | tf_op jit(solution)/shard_map/reduce_scatter | solution.py:261
  (380 shorter events, 107.6 us)
Async XLA Ops:
  7.2 36.3 %all-gather.7.cloned.1.call-start = ((), (), s32[]{:S(2)}) async-start(), calls=%async_computation.8 | async-start | bytes 1769472 | tf_op jit(solution)/shard_map/all_gather | solution.py:192
  16.5 118.3 %all-gather.11.cloned.1.call-start = ((), (), s32[]{:S(2)}) async-start(), calls=%async_computation.13 | async-start | bytes 8912896 | tf_op jit(solution)/shard_map/all_gather | solution.py:211
  18.1 38.1 %copy-start.22 = (s32[96]{0:T(128)}, s32[96]{0:T(128)S(1)}, u32[]{:S(2)}) copy-start(s32[96]{0:T(128)S(1)} %select_reduce_fusion.1) | copy-start | bytes 1156
  18.7 27.5 %all-to-all-start = ((s32[96,16,1]{0,2,1:T(1,128)}), s32[96,16,1]{0,2,1:T(1,128)S(1)}, u32[]{:S(2)}, u32[]{:S(2)}) async-start(s32[96,16,1]{0,2,1:T(1,128)} %broadcast_in_dim.247), calls=%async_computation | async-start | bytes 16384 | tf_op jit(solution)/shard_map/all_to_all | solution.py:221
  26.7 197.8 %all-gather.13.cloned.1.call-start = ((), (), s32[]{:S(2)}) async-start(), calls=%async_computation.14 | async-start | bytes 8912896 | tf_op jit(solution)/shard_map/all_gather | solution.py:236
  46.2 38.5 %all-to-all-start.1 = ((bf16[192,16,256]{2,0,1:T(8,128)(2,1)}), bf16[192,16,256]{2,0,1:T(8,128)(2,1)S(1)}, u32[]{:S(2)}, u32[]{:S(2)}) async-start(bf16[192,16,256]{2,0,1:T(8,128)(2,1)} %bitcast.202), calls=%async_computation.1 | async-start | bytes 3145728 | tf_op jit(solution)/shard_map/all_to_all | solution.py:193
  141.7 18.5 %all-to-all-start.2 = ((bf16[96,16,128]{2,0,1:T(8,128)(2,1)}), bf16[96,16,128]{2,0,1:T(8,128)(2,1)S(1)}, u32[]{:S(2)}, u32[]{:S(2)}) async-start(bf16[96,16,128]{2,0,1:T(8,128)(2,1)} %pad_maximum_fusion), calls=%async_computation.2 | async-start | bytes 786432 | tf_op jit(solution)/shard_map/all_to_all | solution.py:220
  146.7 14.2 %copy-start.10 = (s32[512]{0:T(512)S(1)}, s32[512]{0:T(512)}, u32[]{:S(2)}) copy-start(s32[512]{0:T(512)} %get-tuple-element.1122) | copy-start | bytes 6148
  146.7 14.2 %copy-start.13 = (f32[1,512]{1,0:T(1,128)S(1)}, f32[1,512]{1,0:T(1,128)}, u32[]{:S(2)}) copy-start(f32[1,512]{1,0:T(1,128)} %custom-call.9) | copy-start | bytes 6148
  161.0 20.1 %copy-start.9 = (bf16[512,1,128]{2,0,1:T(8,128)(2,1)S(1)}, bf16[512,1,128]{2,0,1:T(8,128)(2,1)}, u32[]{:S(2)}) copy-start(bf16[512,1,128]{2,0,1:T(8,128)(2,1)} %get-tuple-element.1081) | copy-start | bytes 393220
  161.0 20.1 %copy-start.12 = (f32[1,512]{1,0:T(1,128)S(1)}, f32[1,512]{1,0:T(1,128)}, u32[]{:S(2)}) copy-start(f32[1,512]{1,0:T(1,128)} %custom-call.12) | copy-start | bytes 6148
  181.1 14.7 %copy-start.11 = (f32[1,512]{1,0:T(1,128)S(1)}, f32[1,512]{1,0:T(1,128)}, u32[]{:S(2)}) copy-start(f32[1,512]{1,0:T(1,128)} %custom-call.15) | copy-start | bytes 6148
  211.3 12.9 %all-to-all-start.3 = ((bf16[16,96,128]{2,1,0:T(8,128)(2,1)}), bf16[16,96,128]{2,1,0:T(8,128)(2,1)S(1)}, u32[]{:S(2)}, u32[]{:S(2)}) async-start(bf16[16,96,128]{2,1,0:T(8,128)(2,1)} %bitcast.21), calls=%async_computation.3 | async-start | bytes 786432 | tf_op jit(solution)/shard_map/all_to_all | solution.py:226
  214.9 75.6 %all-reduce.4.cloned.1.call-start = ((), (), s32[]{:S(2)}) async-start(), calls=%async_computation.9 | async-start | bytes 1572864 | tf_op jit(solution)/shard_map/psum | solution.py:242
  229.3 61.2 %copy-start.2 = (bf16[192,2048]{1,0:T(8,128)(2,1)S(1)}, bf16[192,2048]{1,0:T(8,128)(2,1)}, u32[]{:S(2)}) copy-start(bf16[192,2048]{1,0:T(8,128)(2,1)} %param.27) | copy-start | bytes 2359300
  231.1 130.7 %all-gather.9.cloned.1.call-start = ((), (), s32[]{:S(2)}) async-start(), calls=%async_computation.10 | async-start | bytes 6684672 | tf_op jit(solution)/shard_map/all_gather | solution.py:250
  231.8 61.4 %copy-start.21 = (f32[2048]{0:T(1024)S(1)}, f32[2048]{0:T(1024)}, u32[]{:S(2)}) copy-start(f32[2048]{0:T(1024)} %param.33) | copy-start | bytes 24580
  298.1 63.7 %copy-start.33 = (bf16[1,2048,352]{1,2,0:T(8,128)(2,1)S(1)}, bf16[1,2048,352]{1,2,0:T(8,128)(2,1)}, u32[]{:S(2)}) copy-start(bf16[1,2048,352]{1,2,0:T(8,128)(2,1)} %param.35) | copy-start | bytes 4325380
  301.0 67.4 %copy-start.34 = (bf16[1,352,2048]{2,1,0:T(8,128)(2,1)S(1)}, bf16[1,352,2048]{2,1,0:T(8,128)(2,1)}, u32[]{:S(2)}) copy-start(bf16[1,352,2048]{2,1,0:T(8,128)(2,1)} %param.37) | copy-start | bytes 4325380
  301.0 181.2 %reduce-scatter.3.cloned.1.call-start = ((), (), s32[]{:S(2)}) async-start(), calls=%async_computation.11 | async-start | bytes 6684672 | tf_op jit(solution)/shard_map/reduce_scatter | solution.py:254
  381.7 12.8 %all-to-all-start.4 = ((s32[16,1,1]{2,1,0:T(1,128)}), s32[16,1,1]{2,1,0:T(1,128)S(1)}, u32[]{:S(2)}, u32[]{:S(2)}) async-start(s32[16,1,1]{2,1,0:T(1,128)} %copy.66), calls=%async_computation.6 | async-start | bytes 16384 | tf_op jit(solution)/shard_map/all_to_all | solution.py:182
  394.5 90.9 %all-to-all-start.5 = ((bf16[16,128,512]{2,1,0:T(8,128)(2,1)}), bf16[16,128,512]{2,1,0:T(8,128)(2,1)S(1)}, u32[]{:S(2)}, u32[]{:S(2)}) async-start(bf16[16,128,512]{2,1,0:T(8,128)(2,1)} %bitcast.52), calls=%async_computation.7 | async-start | bytes 4194304 | tf_op jit(solution)/shard_map/all_to_all | solution.py:181
  398.2 117.9 %reduce-scatter.5.cloned.1.call-start = ((), (), s32[]{:S(2)}) async-start(), calls=%async_computation.12 | async-start | bytes 884736 | tf_op jit(solution)/shard_map/reduce_scatter | solution.py:261
  486.5 31.3 %copy-start.1 = (bf16[2048,512]{1,0:T(8,128)(2,1)S(1)}, bf16[2048,512]{1,0:T(8,128)(2,1)}, u32[]{:S(2)}) copy-start(bf16[2048,512]{1,0:T(8,128)(2,1)} %param.30) | copy-start | bytes 6291460
  (35 other events, 111.2 us)
Sparse Core Ops, SparseCore 0:
  16.6 26.8 all-gather.6
  45.6 89.1 all-gather.10
  137.0 72.2 all-gather.12
  231.2 59.2 all-reduce.3
  301.1 60.6 all-gather.8
  380.4 101.7 reduce-scatter.2
  485.1 31.0 reduce-scatter.4
where the time goes:
time: 526 us; the launch traced here: 525 us
  waiting for transfers between devices  338 us (64%)
  matrix products  70.3 us (13%)
  local copies, waits for them, and re-layouts  40.2 us (8%)
  starting transfers between devices  32.9 us (6%)
  other arithmetic  26.8 us (5%)
  between operations  15 us (3%)
    reduce_scatter x1, waiting for transfers between devices, shards(): lax.psum_scatter(jnp.dot(hidden, down_weight[0], preferred_element_type=j...  83.9 us
    all_gather x1, waiting for transfers between devices, shards(): portion = lax.all_gather(expert_input, 'tok', axis=0, tiled=True)  60.5 us
    psum x1, waiting for transfers between devices, shards(): lax.psum(attn_rows.astype(jnp.bfloat16), 'exp').astype(jnp.float32)  58.7 us
    all_gather x1, waiting for transfers between devices, shards(): lax.all_gather(query_weight[0], 'tok', axis=1, tiled=True)  43.1 us
    reduce_scatter x1, waiting for transfers between devices, shards(): lax.psum_scatter(expert_local.astype(jnp.bfloat16), 'exp', scatter_dimens...  28.4 us
    all_to_all x1, waiting for transfers between devices, shards(): lax.all_to_all(all_heads.reshape(rows_here, tok_count, heads_here * 2 * h...  25.7 us
    dot_general x18, matrix products, visit(): jnp.einsum('qhd,khd->hqk', query_part, key_part, preferred_element_type=j...  23.6 us
    dot_general x1, matrix products, shards(): jnp.dot(hidden, down_weight[0], preferred_element_type=jnp.float32)  11.9 us
  transfers between devices with their start and end apart: 13, of which 10 were waited for; matrix products, arithmetic and copies ran while one was open for 16% of the time, Pallas kernels for 0%

commit v1 on v0

--- a/solution.py
+++ b/solution.py
@@ -6,6 +6,12 @@
 HD = 128
 PAGE = 128
 epsilon = 1e-06
+
+
+def in_order(blocks, dim):
+    blocks = jnp.moveaxis(blocks, 0, dim)
+    lengths = blocks.shape
+    return blocks.reshape(*lengths[:dim], lengths[dim] * lengths[dim + 1], *lengths[dim + 2 :])
 
 
 def normalize(values, gain):
@@ -189,7 +195,19 @@
         .astype(jnp.bfloat16)
         .reshape(slot_count, page_rows, -1)
     )
-    all_heads = lax.all_gather(paired, "exp", axis=1, tiled=True)
+    devices = lax.axis_size("exp")
+    pairs = [(i, (i + 1) % devices) for i in range(devices)]
+    back = [(b, a) for a, b in pairs]
+    lower, upper = ([], [])
+    for step in range(devices - 1):
+        if step % 2 == 0:
+            lower.append(lax.ppermute(lower[-1] if lower else paired, "exp", pairs))
+        else:
+            upper.append(lax.ppermute(upper[-1] if upper else paired, "exp", back))
+    blocks = jnp.stack([*lower[::-1], paired, *upper])
+    shift = lax.axis_index("exp") - len(lower)
+    blocks = blocks[(jnp.arange(devices) - shift) % devices]
+    all_heads = in_order(blocks, 1)
     regrouped = lax.all_to_all(
         all_heads.reshape(rows_here, tok_count, heads_here * 2 * head_size),
         "tok",

time: 526 us -> 499 us (0.949)
  waiting for transfers between devices: 338 us -> 301 us
  starting transfers between devices: 32.9 us -> 41.8 us
    all_gather x1, waiting for transfers between devices: 43.1 us -> 4.45 us  [shards(): lax.all_gather(query_weight[0], 'tok', axis=1, tiled=True)]
    ppermute x0 -> x7, waiting for transfers between devices: none -> 12.5 us  [the longest x4 12.4 us: shards(): lower.append(lax.ppermute(lower[-1] if lower else paired, 'exp', pairs))]
    all_gather x1 -> x0, waiting for transfers between devices: 11.2 us -> none  [shards(): all_heads = lax.all_gather(paired, 'exp', axis=1, tiled=True)]
    ppermute x0 -> x7, starting transfers between devices: none -> 9.06 us  [the longest x3 9.02 us: shards(): upper.append(lax.ppermute(upper[-1] if upper else paired, 'exp', back))]
  transfers between devices with their start and end apart: 13 -> 19, of which waited for: 10 -> 12; matrix products, arithmetic and copies ran while one was open for 16% -> 19% of each run, Pallas kernels for 0% -> 0%
where the time goes in v1:
time: 499 us; the launch traced here: 498 us
  waiting for transfers between devices  301 us (60%)
  matrix products  70.8 us (14%)
  local copies, waits for them, and re-layouts  43.6 us (9%)
  starting transfers between devices  41.8 us (8%)
  other arithmetic  25.2 us (5%)
  between operations  14.8 us (3%)
    reduce_scatter x1, waiting for transfers between devices, shards(): lax.psum_scatter(jnp.dot(hidden, down_weight[0], preferred_element_type=j...  83.7 us
    psum x1, waiting for transfers between devices, shards(): lax.psum(attn_rows.astype(jnp.bfloat16), 'exp').astype(jnp.float32)  61.8 us
    all_gather x1, waiting for transfers between devices, shards(): portion = lax.all_gather(expert_input, 'tok', axis=0, tiled=True)  60.7 us
    reduce_scatter x1, waiting for transfers between devices, shards(): lax.psum_scatter(expert_local.astype(jnp.bfloat16), 'exp', scatter_dimens...  28.4 us
    dot_general x18, matrix products, visit(): jnp.einsum('qhd,khd->hqk', query_part, key_part, preferred_element_type=j...  23.7 us
    all_to_all x1, waiting for transfers between devices, shards(): lax.all_to_all(all_heads.reshape(rows_here, tok_count, heads_here * 2 * h...  23 us
    ppermute x4, waiting for transfers between devices, shards(): lower.append(lax.ppermute(lower[-1] if lower else paired, 'exp', pairs))  12.4 us
    dot_general x1, matrix products, shards(): jnp.dot(hidden, down_weight[0], preferred_element_type=jnp.float32)  11.9 us
  transfers between devices with their start and end apart: 19, of which 12 were waited for; matrix products, arithmetic and copies ran while one was open for 19% of the time, Pallas kernels for 0%

profile of v1, /device:TPU:0, one launch (start us, length us, event | category | flops | bytes accessed | tf_op | source)
XLA Modules:
  0.0 497.8 jit_solution(1079210512942588770)
XLA Ops:
  19.7 8.0 %all-to-all-start = ((s32[96,16,1]{0,2,1:T(1,128)}), s32[96,16,1]{0,2,1:T(1,128)S(1)}, u32[]{:S(2)}, u32[]{:S(2)}) async-start(s32[96,16,1]{0,2,1:T(1,128)} %broadcast_in_dim.248), calls=%async_computation | async-start | bytes 16384 | tf_op jit(solution)/shard_map/all_to_all | solution.py:239
  32.6 6.2 %collective-permute-done.1 = bf16[192,512]{1,0:T(8,128)(2,1)S(1)} collective-permute-done((bf16[192,512]{1,0:T(8,128)(2,1)S(1)}, bf16[192,512]{1,0:T(8,128)(2,1)S(1)}, u32[]{:S(2)}, u32[]{:S(2)}) %collective-permute-start.1) | collective-permute-done | bytes 196640 | tf_op jit(solution)/shard_map/ppermute | solution.py:204
  60.8 7.2 %all-to-all-start.1 = ((bf16[192,16,256]{2,0,1:T(8,128)(2,1)}), bf16[192,16,256]{2,0,1:T(8,128)(2,1)S(1)}, u32[]{:S(2)}, u32[]{:S(2)}) async-start(bf16[192,16,256]{2,0,1:T(8,128)(2,1)} %copy.56), calls=%async_computation.1 | async-start | bytes 3145728 | tf_op jit(solution)/shard_map/all_to_all | solution.py:211
  72.1 23.0 %all-to-all-done.1 = bf16[192,16,256]{2,0,1:T(8,128)(2,1)S(1)} async-done(((bf16[192,16,256]{2,0,1:T(8,128)(2,1)}), bf16[192,16,256]{2,0,1:T(8,128)(2,1)S(1)}, u32[]{:S(2)}, u32[]{:S(2)}) %all-to-all-start.1) | async-done | bytes 1572896 | tf_op jit(solution)/shard_map/all_to_all | solution.py:211
  98.7 3.5 fusion.141
  102.2 4.5 all-gather.8.cloned.1.call-done
  106.6 4.9 fusion.84
  113.5 4.5 all-to-all-start.2
  120.7 9.9 %all-to-all-done.2 = bf16[96,16,128]{2,0,1:T(8,128)(2,1)S(1)} async-done(((bf16[96,16,128]{2,0,1:T(8,128)(2,1)}), bf16[96,16,128]{2,0,1:T(8,128)(2,1)S(1)}, u32[]{:S(2)}, u32[]{:S(2)}) %all-to-all-start.2) | async-done | bytes 393248 | tf_op jit(solution)/shard_map/all_to_all | solution.py:238
  131.3 18.7 %while.54 = (s32[]{:T(128)}, f32[1,512]{1,0:T(1,128)S(1)}, f32[1,512]{1,0:T(1,128)S(1)}, f32[1,512,128]{2,1,0:T(8,128)}, s32[3072]{0:T(1024)S(1)}, /*index=5*/s3...) while((s32[]{:T(128)}, f32[1,512]{1,0:T(1,128)S(1)}, ...), condition=%wide.region_14.16_spmd.clone, body=%wide.region_11.15_spmd.clone.sunk | while | flops 139135488 | bytes 6226191 | solution.py:122
  151.1 15.0 %while.55 = (s32[]{:T(128)}, f32[1,512]{1,0:T(1,128)S(1)}, f32[1,512]{1,0:T(1,128)S(1)}, f32[1,512,128]{2,1,0:T(8,128)S(1)}, s32[3072]{0:T(1024)S(1)}, /*index=5...) while((s32[]{:T(128)}, f32[1,512]{1,0:T(1,128)S(1)}, ...), condition=%wide.region_18.20_spmd.clone, body=%wide.region_15.19_spmd.clone.sunk | while | flops 139135488 | bytes 4128983 | solution.py:122
  166.3 14.5 %while.56 = (s32[]{:T(128)}, f32[1,512]{1,0:T(1,128)S(1)}, f32[1,512]{1,0:T(1,128)S(1)}, f32[1,512,128]{2,1,0:T(8,128)S(1)}, s32[3072]{0:T(1024)S(1)}, /*index=5...) while((s32[]{:T(128)}, f32[1,512]{1,0:T(1,128)S(1)}, ...), condition=%wide.region_22.24_spmd.clone, body=%wide.region_19.23_spmd.clone.sunk | while | flops 139135488 | bytes 4128983 | solution.py:122
  181.7 3.6 all-to-all-start.3
  185.5 9.2 %all-to-all-done.3 = bf16[16,96,128]{2,1,0:T(8,128)(2,1)S(1)} async-done(((bf16[16,96,128]{2,1,0:T(8,128)(2,1)}), bf16[16,96,128]{2,1,0:T(8,128)(2,1)S(1)}, u32[]{:S(2)}, u32[]{:S(2)}) %all-to-all-start.3) | async-done | bytes 393248 | tf_op jit(solution)/shard_map/all_to_all | solution.py:244
  194.8 4.8 fusion.74
  202.4 61.8 %all-reduce.4.cloned.1.call-done = bf16[192,2048]{1,0:T(8,128)(2,1)} async-done(((bf16[192,2048]{1,0:T(8,128)(2,1)}), bf16[192,2048]{1,0:T(8,128)(2,1)}) %all-reduce.4.cloned.1.call-update) | async-done | bytes 786448 | tf_op jit(solution)/shard_map/psum | solution.py:260
  274.7 60.7 %all-gather.6.cloned.1.call-done = bf16[1536,2048]{1,0:T(8,128)(2,1)} async-done(((bf16[96,2048]{1,0:T(8,128)(2,1)}), bf16[1536,2048]{1,0:T(8,128)(2,1)}) %all-gather.6.cloned.1.call-update) | async-done | bytes 6291472 | tf_op jit(solution)/shard_map/all_gather | solution.py:268
  335.4 7.0 %fusion.82 = f32[1536,352]{0,1:T(8,128)} fusion(bf16[1536,2048]{1,0:T(8,128)(2,1)} %all-gather.6.cloned.1.call-done, bf16[1,2048,352]{1,2,0:T(8,128)(2,1)} %param.35), kind=kOutput, calls=%fused_computation.123 | convolution fusion | flops 2214592512 | bytes 9895936 | tf_op jit(solution)/shard_map/dot_general | solution.py:269
  342.4 11.9 %convolution_convert_fusion.1 = bf16[1536,2048]{1,0:T(8,128)(2,1)} fusion(bf16[1,352,2048]{2,1,0:T(8,128)(2,1)S(1)} %copy-done.15, bf16[1536,2048]{1,0:T(8,128)(2,1)} %all-gather.6.cloned.1.call-done, f32[1536,352]{0,1:T(8,128)} %fusion.82, bf16[1,2048,352]{1,2,0:T(8,128)(2,1)} %param.36), kind=kOutput, calls=%fused_computation.105 | convolution fusion | flops 4435574784 | bytes 17629184 | tf_op jit(solution)/shard_map/dot_general | solution.py:273
  355.0 5.3 %all-to-all-start.4 = ((s32[16,1,1]{2,1,0:T(1,128)}), s32[16,1,1]{2,1,0:T(1,128)S(1)}, u32[]{:S(2)}, u32[]{:S(2)}) async-start(s32[16,1,1]{2,1,0:T(1,128)} %copy.62), calls=%async_computation.6 | async-start | bytes 16384 | tf_op jit(solution)/shard_map/all_to_all | solution.py:188
  362.4 5.4 %all-to-all-done.4 = s32[16,1,1]{2,1,0:T(1,128)S(1)} async-done(((s32[16,1,1]{2,1,0:T(1,128)}), s32[16,1,1]{2,1,0:T(1,128)S(1)}, u32[]{:S(2)}, u32[]{:S(2)}) %all-to-all-start.4) | async-done | bytes 96 | tf_op jit(solution)/shard_map/all_to_all | solution.py:188
  367.8 3.7 all-to-all-start.5
  371.6 83.7 %reduce-scatter.3.cloned.1.call-done = bf16[96,2048]{1,0:T(8,128)(2,1)} async-done(((bf16[1536,2048]{1,0:T(8,128)(2,1)}), bf16[96,2048]{1,0:T(8,128)(2,1)}) %reduce-scatter.3.cloned.1.call-update) | async-done | bytes 393232 | tf_op jit(solution)/shard_map/reduce_scatter | solution.py:272
  460.9 28.4 %reduce-scatter.5.cloned.1.call-done = bf16[192,256]{1,0:T(8,128)(2,1)} async-done(((bf16[192,2048]{1,0:T(8,128)(2,1)}), bf16[192,256]{1,0:T(8,128)(2,1)}) %reduce-scatter.5.cloned.1.call-update) | async-done | bytes 98320 | tf_op jit(solution)/shard_map/reduce_scatter | solution.py:279
  (364 shorter events, 124.7 us)
Async XLA Ops:
  7.2 99.5 %all-gather.8.cloned.1.call-start = ((), (), s32[]{:S(2)}) async-start(), calls=%async_computation.12 | async-start | bytes 8912896 | tf_op jit(solution)/shard_map/all_gather | solution.py:229
  15.3 17.2 %collective-permute-start = (bf16[192,512]{1,0:T(8,128)(2,1)S(1)}, bf16[192,512]{1,0:T(8,128)(2,1)S(1)}, u32[]{:S(2)}, u32[]{:S(2)}) collective-permute-start(bf16[192,512]{1,0:T(8,128)(2,1)S(1)} %convert_element_type.136), channel_id=1, source_target_pairs={{0,1},{1,2},{2,3},{3,4},{4,5},{5,6},{6,7},{7,0},{8,9},{9,10},{10,1... | collective-permute-start | bytes 589832 | tf_op jit(solution)/shard_map/ppermute | solution.py:204
  15.3 23.7 %collective-permute-start.4 = (bf16[192,512]{1,0:T(8,128)(2,1)S(1)}, bf16[192,512]{1,0:T(8,128)(2,1)S(1)}, u32[]{:S(2)}, u32[]{:S(2)}) collective-permute-start(bf16[192,512]{1,0:T(8,128)(2,1)S(1)} %convert_element_type.136), channel_id=1, source_target_pairs={{1,0},{2,1},{3,2},{4,3},{5,4},{6,5},{7,6},{0,7},{9,8},{10,9},{11,1... | collective-permute-start | bytes 589832 | tf_op jit(solution)/shard_map/ppermute | solution.py:206
  19.7 41.1 %all-to-all-start = ((s32[96,16,1]{0,2,1:T(1,128)}), s32[96,16,1]{0,2,1:T(1,128)S(1)}, u32[]{:S(2)}, u32[]{:S(2)}) async-start(s32[96,16,1]{0,2,1:T(1,128)} %broadcast_in_dim.248), calls=%async_computation | async-start | bytes 16384 | tf_op jit(solution)/shard_map/all_to_all | solution.py:239
  27.7 167.1 %all-gather.10.cloned.1.call-start = ((), (), s32[]{:S(2)}) async-start(), calls=%async_computation.13 | async-start | bytes 8912896 | tf_op jit(solution)/shard_map/all_gather | solution.py:254
  32.5 6.3 %collective-permute-start.1 = (bf16[192,512]{1,0:T(8,128)(2,1)S(1)}, bf16[192,512]{1,0:T(8,128)(2,1)S(1)}, u32[]{:S(2)}, u32[]{:S(2)}) collective-permute-start(bf16[192,512]{1,0:T(8,128)(2,1)S(1)} %collective-permute-done), channel_id=1, source_target_pairs={{0,1},{1,2},{2,3},{3,4},{4,5},{5,6},{6,7},{7,0},{8,9},{9,10},{10,1... | collective-permute-start | bytes 589832 | tf_op jit(solution)/shard_map/ppermute | solution.py:204
  38.8 6.3 %collective-permute-start.2 = (bf16[192,512]{1,0:T(8,128)(2,1)S(1)}, bf16[192,512]{1,0:T(8,128)(2,1)S(1)}, u32[]{:S(2)}, u32[]{:S(2)}) collective-permute-start(bf16[192,512]{1,0:T(8,128)(2,1)S(1)} %collective-permute-done.1), channel_id=1, source_target_pairs={{0,1},{1,2},{2,3},{3,4},{4,5},{5,6},{6,7},{7,0},{8,9},{9,10},{10,1... | collective-permute-start | bytes 589832 | tf_op jit(solution)/shard_map/ppermute | solution.py:204
  39.0 6.2 %collective-permute-start.5 = (bf16[192,512]{1,0:T(8,128)(2,1)S(1)}, bf16[192,512]{1,0:T(8,128)(2,1)S(1)}, u32[]{:S(2)}, u32[]{:S(2)}) collective-permute-start(bf16[192,512]{1,0:T(8,128)(2,1)S(1)} %collective-permute-done.4), channel_id=1, source_target_pairs={{1,0},{2,1},{3,2},{4,3},{5,4},{6,5},{7,6},{0,7},{9,8},{10,9},{11,1... | collective-permute-start | bytes 589832 | tf_op jit(solution)/shard_map/ppermute | solution.py:206
  45.1 6.3 %collective-permute-start.3 = (bf16[192,512]{1,0:T(8,128)(2,1)S(1)}, bf16[192,512]{1,0:T(8,128)(2,1)S(1)}, u32[]{:S(2)}, u32[]{:S(2)}) collective-permute-start(bf16[192,512]{1,0:T(8,128)(2,1)S(1)} %collective-permute-done.2), channel_id=1, source_target_pairs={{0,1},{1,2},{2,3},{3,4},{4,5},{5,6},{6,7},{7,0},{8,9},{9,10},{10,1... | collective-permute-start | bytes 589832 | tf_op jit(solution)/shard_map/ppermute | solution.py:204
  45.2 6.4 %collective-permute-start.6 = (bf16[192,512]{1,0:T(8,128)(2,1)S(1)}, bf16[192,512]{1,0:T(8,128)(2,1)S(1)}, u32[]{:S(2)}, u32[]{:S(2)}) collective-permute-start(bf16[192,512]{1,0:T(8,128)(2,1)S(1)} %collective-permute-done.5), channel_id=1, source_target_pairs={{1,0},{2,1},{3,2},{4,3},{5,4},{6,5},{7,6},{0,7},{9,8},{10,9},{11,1... | collective-permute-start | bytes 589832 | tf_op jit(solution)/shard_map/ppermute | solution.py:206
  60.8 34.4 %all-to-all-start.1 = ((bf16[192,16,256]{2,0,1:T(8,128)(2,1)}), bf16[192,16,256]{2,0,1:T(8,128)(2,1)S(1)}, u32[]{:S(2)}, u32[]{:S(2)}) async-start(bf16[192,16,256]{2,0,1:T(8,128)(2,1)} %copy.56), calls=%async_computation.1 | async-start | bytes 3145728 | tf_op jit(solution)/shard_map/all_to_all | solution.py:211
  113.5 17.1 %all-to-all-start.2 = ((bf16[96,16,128]{2,0,1:T(8,128)(2,1)}), bf16[96,16,128]{2,0,1:T(8,128)(2,1)S(1)}, u32[]{:S(2)}, u32[]{:S(2)}) async-start(bf16[96,16,128]{2,0,1:T(8,128)(2,1)} %pad_maximum_fusion), calls=%async_computation.2 | async-start | bytes 786432 | tf_op jit(solution)/shard_map/all_to_all | solution.py:238
  131.3 19.8 %copy-start.6 = (f32[1,512,128]{2,1,0:T(8,128)S(1)}, f32[1,512,128]{2,1,0:T(8,128)}, u32[]{:S(2)}) copy-start(f32[1,512,128]{2,1,0:T(8,128)} %custom-call.13) | copy-start | bytes 786436
  181.7 12.9 %all-to-all-start.3 = ((bf16[16,96,128]{2,1,0:T(8,128)(2,1)}), bf16[16,96,128]{2,1,0:T(8,128)(2,1)S(1)}, u32[]{:S(2)}, u32[]{:S(2)}) async-start(bf16[16,96,128]{2,1,0:T(8,128)(2,1)} %bitcast.30), calls=%async_computation.3 | async-start | bytes 786432 | tf_op jit(solution)/shard_map/all_to_all | solution.py:244
  185.3 78.8 %all-reduce.4.cloned.1.call-start = ((), (), s32[]{:S(2)}) async-start(), calls=%async_computation.8 | async-start | bytes 1572864 | tf_op jit(solution)/shard_map/psum | solution.py:260
  199.7 64.5 %copy-start.2 = (bf16[192,2048]{1,0:T(8,128)(2,1)S(1)}, bf16[192,2048]{1,0:T(8,128)(2,1)}, u32[]{:S(2)}) copy-start(bf16[192,2048]{1,0:T(8,128)(2,1)} %param.27) | copy-start | bytes 2359300
  201.4 134.0 %all-gather.6.cloned.1.call-start = ((), (), s32[]{:S(2)}) async-start(), calls=%async_computation.9 | async-start | bytes 6684672 | tf_op jit(solution)/shard_map/all_gather | solution.py:268
  202.3 64.4 %copy-start.13 = (f32[2048]{0:T(1024)S(1)}, f32[2048]{0:T(1024)}, u32[]{:S(2)}) copy-start(f32[2048]{0:T(1024)} %param.33) | copy-start | bytes 24580
  274.6 67.8 %copy-start.15 = (bf16[1,352,2048]{2,1,0:T(8,128)(2,1)S(1)}, bf16[1,352,2048]{2,1,0:T(8,128)(2,1)}, u32[]{:S(2)}) copy-start(bf16[1,352,2048]{2,1,0:T(8,128)(2,1)} %param.37) | copy-start | bytes 4325380
  274.6 180.7 %reduce-scatter.3.cloned.1.call-start = ((), (), s32[]{:S(2)}) async-start(), calls=%async_computation.10 | async-start | bytes 6684672 | tf_op jit(solution)/shard_map/reduce_scatter | solution.py:272
  355.0 12.8 %all-to-all-start.4 = ((s32[16,1,1]{2,1,0:T(1,128)}), s32[16,1,1]{2,1,0:T(1,128)S(1)}, u32[]{:S(2)}, u32[]{:S(2)}) async-start(s32[16,1,1]{2,1,0:T(1,128)} %copy.62), calls=%async_computation.6 | async-start | bytes 16384 | tf_op jit(solution)/shard_map/all_to_all | solution.py:188
  367.8 90.7 %all-to-all-start.5 = ((bf16[16,128,512]{2,1,0:T(8,128)(2,1)}), bf16[16,128,512]{2,1,0:T(8,128)(2,1)S(1)}, u32[]{:S(2)}, u32[]{:S(2)}) async-start(bf16[16,128,512]{2,1,0:T(8,128)(2,1)} %bitcast.61), calls=%async_computation.7 | async-start | bytes 4194304 | tf_op jit(solution)/shard_map/all_to_all | solution.py:187
  371.6 117.7 %reduce-scatter.5.cloned.1.call-start = ((), (), s32[]{:S(2)}) async-start(), calls=%async_computation.11 | async-start | bytes 884736 | tf_op jit(solution)/shard_map/reduce_scatter | solution.py:279
  459.7 31.3 %copy-start.1 = (bf16[2048,512]{1,0:T(8,128)(2,1)S(1)}, bf16[2048,512]{1,0:T(8,128)(2,1)}, u32[]{:S(2)}) copy-start(bf16[2048,512]{1,0:T(8,128)(2,1)} %param.30) | copy-start | bytes 6291460
  (22 other events, 64.3 us)
Sparse Core Ops, SparseCore 0:
  10.1 96.5 all-gather.7
  108.8 74.2 all-gather.9
  201.5 62.5 all-reduce.3
  274.7 60.6 all-gather.5
  354.4 100.8 reduce-scatter.2
  458.2 31.0 reduce-scatter.4
